TPU v7x, 256 devices: a whole 4x4x8 slice. The times are simulated.
256 devices in a mesh: gx: 16 (over x, y_lo, core), gy: 16 (over y_hi, z).
Axes of the slice: x: 4, y: 4 (y_hi: 2, y_lo: 2; y = y_hi * 2 + y_lo), z: 8, core: 2. Of those that a mesh axis runs over, the one named last changes fastest.
Arguments:
- object_field: float32 [2, 1024, 1024], P(None, 'gy', 'gx'), may hold values from -1 to 1
- probe_modes: float32 [2, 1024, 128], P(None, ('gy', 'gx')), may hold values from -1.5 to 1.5
- positions: int32 [16, 16, 12, 2], P('gy', 'gx'), may hold values from 4 to 60, as said below
- amplitudes: float32 [16, 16, 12, 128, 128], P('gy', 'gx'), may hold values from 0 to 2
Outputs:
- object_out: float32 [2, 1024, 1024], P(None, 'gy', 'gx')
- probe_out: float32 [2, 1024, 128], P(None, ('gy', 'gx'))
Inputs may be any that keep to these rules, and one draw needn't show every extreme that they name: `positions`: each entry is a (row, column) inside its own tile; the centres of one tile lie at distinct cells of the 16 grid, each moved from the cell's middle by at most 4 cells along each dimension.
All inputs are finite; a program needn't handle non-finite values.
Results may differ from a plain program's by a relative error of at most 0.00065.
The roundings to bfloat16 on the way count: a program that leaves them out, or rounds other values in their place, can miss the bound.
Values sent between devices are 32-bit elements; how exact they have to be, the bound alone decides.
No kernel may reach another device: no remote copies, remote signals or barrier semaphores. Data moves between devices by JAX's collectives and lax.ppermute only.
A program may use at most 64 MiB of HBM per device.

v0:
```python
import math
import jax
import jax.numpy as jnp
from jax import lax
from jax.sharding import PartitionSpec as P

MODES = 8
ITERS = 2
SOFT_FLOOR = 0.05
OBJECT_REG = 1.0
PROBE_REG = 1.0


def from_behind(block, axis, distance):
    devices = range(lax.axis_size(axis))
    route = [(i - distance, i) for i in devices if i - distance in devices]
    return lax.ppermute(block, axis, route)


def extended_2(array, sides, width):
    for axis, dim in sides:
        peers, length = (lax.axis_size(axis), array.shape[dim])
        up = [(i, (i + 1) % peers) for i in range(peers - 1)]
        down = [(j, i) for i, j in up]
        last = lax.slice_in_dim(array, length - width, length, axis=dim)
        initial = lax.slice_in_dim(array, 0, width, axis=dim)
        before = lax.ppermute(last, axis, up)
        after = lax.ppermute(initial, axis, down)
        array = jnp.concatenate([before, array, after], axis=dim)
    return array


def tables(probe_side, sign_flip):
    indices = jnp.arange(probe_side, dtype=jnp.int32)
    phases = indices[:, None] * indices[None, :] % probe_side
    angles = phases.astype(jnp.float32) * (2.0 * math.pi / probe_side)
    factor = 1.0 / math.sqrt(probe_side)
    cosine = jnp.cos(angles) * factor
    sine_part = sign_flip * jnp.sin(angles) * factor
    left_op = jnp.stack(
        [jnp.stack([cosine, -sine_part]), jnp.stack([sine_part, cosine])]
    ).transpose(0, 2, 1, 3)
    right_op = jnp.stack(
        [jnp.stack([cosine, sine_part]), jnp.stack([-sine_part, cosine])]
    ).transpose(0, 2, 1, 3)
    return (left_op.astype(jnp.bfloat16), right_op.astype(jnp.bfloat16))


def transform(signal, operators):
    left_op, right_op = operators
    halfway = jnp.einsum(
        "dpcr,crmq->dpmq", left_op, signal, preferred_element_type=jnp.float32
    ).astype(jnp.bfloat16)
    return jnp.einsum("crmq,cqdk->drmk", halfway, right_op, preferred_element_type=jnp.float32)


def position_terms(patch_obj, probe, measured, forward, inverse):
    obj_real = patch_obj[0][:, None, :]
    obj_imag = patch_obj[1][:, None, :]
    wave_real = probe[0] * obj_real - probe[1] * obj_imag
    wave_imag = probe[0] * obj_imag + probe[1] * obj_real
    signal = jnp.stack([wave_real, wave_imag]).astype(jnp.bfloat16)
    spectrum = transform(signal, forward)
    intensity = jnp.sum(spectrum[0] * spectrum[0] + spectrum[1] * spectrum[1], axis=1)
    shrink = 1.0 - measured / jnp.sqrt(intensity + SOFT_FLOOR)
    residual = (spectrum * shrink[None, :, None, :]).astype(jnp.bfloat16)
    change = transform(residual, inverse)
    grad_real = jnp.sum(probe[0] * change[0] + probe[1] * change[1], axis=1)
    grad_imag = jnp.sum(probe[0] * change[1] - probe[1] * change[0], axis=1)
    probe_real = obj_real * change[0] + obj_imag * change[1]
    probe_imag = obj_real * change[1] - obj_imag * change[0]
    weight_probe = patch_obj[0] * patch_obj[0] + patch_obj[1] * patch_obj[1]
    return (jnp.stack([grad_real, grad_imag]), jnp.stack([probe_real, probe_imag]), weight_probe)


def fold_rows(gradient, margin, tile_side):
    extent = gradient.shape[1]
    for direction in (1, -1):
        rim_part = gradient[:, extent - margin :, :] if direction == 1 else gradient[:, :margin, :]
        offset = margin if direction == 1 else tile_side
        arrived = from_behind(rim_part, "gy", direction)
        gradient = gradient.at[:, offset : offset + margin, :].add(arrived)
    return gradient[:, margin : margin + tile_side, :]


def fold_cols(gradient, margin, tile_side):
    extent = gradient.shape[2]
    for direction in (1, -1):
        rim_part = gradient[:, :, extent - margin :] if direction == 1 else gradient[:, :, :margin]
        offset = margin if direction == 1 else tile_side
        arrived = from_behind(rim_part, "gx", direction)
        gradient = gradient.at[:, :, offset : offset + margin].add(arrived)
    return gradient[:, :, margin : margin + tile_side]


def unpack_probe(probe_rows, probe_side):
    return probe_rows.reshape(2, MODES, probe_side, probe_side).transpose(0, 2, 1, 3)


def local(object_field, probe_modes, positions, amplitudes):
    probe_side = amplitudes.shape[-1]
    margin = probe_side // 2
    tile_side = object_field.shape[1]
    centres = positions.reshape(-1, 2)
    measured_all = amplitudes.reshape(-1, probe_side, probe_side)
    forward = tables(probe_side, -1.0)
    inverse = tables(probe_side, 1.0)
    gathered = lax.all_gather(probe_modes, ("gy", "gx"), axis=1, tiled=True)
    probe = unpack_probe(gathered, probe_side)
    own_rows = probe_modes
    current = object_field
    for iteration in range(ITERS):
        extended = extended_2(current, (("gy", 1), ("gx", 2)), margin)
        weight_obj = jnp.sum(probe[0] * probe[0] + probe[1] * probe[1], axis=1)

        def visit(running, visit_item):
            grad_obj, grad_probe, weight_probe = running
            row_at, col_at, measured = visit_item
            zero_index = jnp.int32(0)
            patch_obj = lax.dynamic_slice(
                extended, (zero_index, row_at, col_at), (2, probe_side, probe_side)
            )
            g_obj, g_probe, w_probe = position_terms(patch_obj, probe, measured, forward, inverse)
            stacked = jnp.concatenate([g_obj, weight_obj[None]], axis=0)
            before = lax.dynamic_slice(
                grad_obj, (zero_index, row_at, col_at), (3, probe_side, probe_side)
            )
            grad_obj = lax.dynamic_update_slice(
                grad_obj, before + stacked, (zero_index, row_at, col_at)
            )
            return ((grad_obj, grad_probe + g_probe, weight_probe + w_probe), None)

        initial = (
            jnp.zeros((3, tile_side + probe_side, tile_side + probe_side), jnp.float32),
            jnp.zeros((2, probe_side, MODES, probe_side), jnp.float32),
            jnp.zeros((probe_side, probe_side), jnp.float32),
        )
        (grad_obj, grad_probe, weight_probe), _ = lax.scan(
            visit, initial, (centres[:, 0], centres[:, 1], measured_all)
        )
        folded = fold_cols(fold_rows(grad_obj, margin, tile_side), margin, tile_side)
        new_object = current - folded[0:2] / (folded[2] + OBJECT_REG)
        grad_rows = grad_probe.transpose(0, 2, 1, 3).reshape(2, MODES * probe_side, probe_side)
        totals, weight_total = lax.psum((grad_rows, weight_probe), ("gy", "gx"))
        whole_probe = probe.transpose(0, 2, 1, 3)
        whole_probe = whole_probe - totals.reshape(2, MODES, probe_side, probe_side) / (
            weight_total[None, None] + PROBE_REG
        )
        whole_probe = whole_probe.reshape(2, MODES * probe_side, probe_side)
        probe = unpack_probe(whole_probe, probe_side)
        row_count = own_rows.shape[1]
        own_rows = lax.dynamic_slice_in_dim(
            whole_probe, lax.axis_index(("gy", "gx")) * row_count, row_count, 1
        )
        current = new_object
    return (current, own_rows)


def solution(mesh):
    return jax.shard_map(
        local,
        mesh=mesh,
        in_specs=(
            P(None, "gy", "gx"),
            P(None, ("gy", "gx"), None),
            P("gy", "gx", None, None),
            P("gy", "gx", None, None, None),
        ),
        out_specs=(P(None, "gy", "gx"), P(None, ("gy", "gx"), None)),
        check_vma=False,
    )
```

profile of v0, /device:TPU:16, one launch (start us, length us, event | category | flops | bytes accessed | tf_op | source)
XLA Modules:
  0.0 1355.4 jit_solution(5158283582343708737)
XLA Ops:
  8.6 3.8 collective-permute-start
  12.4 5.6 collective-permute-start.1
  24.8 3.6 collective-permute-done.3
  29.3 362.2 %all-gather.2.cloned.1.call-done = f32[2,1024,128]{2,0,1:T(2,128)} async-done(((f32[2,4,128]{2,0,1:T(2,128)}), f32[2,1024,128]{2,0,1:T(2,128)}) %all-gather.2.cloned.1.call-update) | async-done | bytes 1048592 | tf_op jit(solution)/shard_map/all_gather | solution.py:108
  394.4 205.2 %while.38 = (s32[]{:T(128)}, f32[3,192,192]{2,1,0:T(8,128)}, f32[2,128,8,128]{3,1,0,2:T(8,128)}, f32[128,128]{1,0:T(8,128)}, s32[12]{0:T(128)S(1)}, /*index=5*/s...) while((s32[]{:T(128)}, f32[3,192,192]{2,1,0:T(8,128)}, ...), condition=%wide.region_5.6_spmd.clone, body=%wide.region_1.5_spmd.clone.sunk | while | flops 543391744 | bytes 27918840 | solution.py:138
  424.9 2.8 dynamic_update_slice.10
  442.0 2.8 dynamic_update_slice.10
  459.2 2.8 dynamic_update_slice.10
  493.3 2.8 dynamic_update_slice.10
  510.4 2.8 dynamic_update_slice.10
  527.6 2.8 dynamic_update_slice.10
  544.6 2.8 dynamic_update_slice.10
  578.8 2.9 dynamic_update_slice.10
  596.0 2.8 dynamic_update_slice.10
  600.7 2.8 collective-permute-start.4
  603.5 6.7 collective-permute-start.5
  610.2 3.1 collective-permute-done.4
  623.0 7.7 collective-permute-start.9
  632.6 4.0 collective-permute-start.10
  637.9 3.2 collective-permute-done.11
  642.1 236.9 %all-reduce.7.cloned.1.call-done = (f32[2,1024,128]{2,0,1:T(2,128)}, f32[128,128]{1,0:T(8,128)}) async-done(((f32[2,1024,128]{2,0,1:T(2,128)}, f32[128,128]{1,0:T(8,128)}), (f32[2,1024,128]{2,0,1:T(2,128)}, f32[128,128]{1,0:T(8,128)})) %all-reduce.7.cloned.1.call-update) | async-done | bytes 1114128 | tf_op jit(solution)/shard_map/psum | solution.py:144
  882.9 197.0 %while.39 = (s32[]{:T(128)}, f32[3,192,192]{2,1,0:T(8,128)}, f32[2,128,8,128]{3,1,0,2:T(8,128)}, f32[128,128]{1,0:T(8,128)}, s32[12]{0:T(128)S(1)}, /*index=5*/s...) while((s32[]{:T(128)}, f32[3,192,192]{2,1,0:T(8,128)}, ...), condition=%wide.region_13.14_spmd.clone, body=%wide.region_9.13_spmd.clone.sunk | while | flops 543391744 | bytes 27918840 | solution.py:138
  928.4 2.8 dynamic_update_slice.11
  977.7 2.8 dynamic_update_slice.11
  994.2 2.8 dynamic_update_slice.11
  1027.0 2.8 dynamic_update_slice.11
  1059.8 2.9 dynamic_update_slice.11
  1076.3 2.8 dynamic_update_slice.11
  1082.9 7.5 collective-permute-start.13
  1090.4 3.0 copy.30
  1097.3 3.0 collective-permute-done.15
  1101.9 244.8 %all-reduce.5.cloned.1.call-done = (f32[2,1024,128]{2,0,1:T(2,128)}, f32[128,128]{1,0:T(8,128)}) async-done(((f32[2,1024,128]{2,0,1:T(2,128)}, f32[128,128]{1,0:T(8,128)}), (f32[2,1024,128]{2,0,1:T(2,128)}, f32[128,128]{1,0:T(8,128)})) %all-reduce.5.cloned.1.call-update) | async-done | bytes 1114128 | tf_op jit(solution)/shard_map/psum | solution.py:144
  (705 shorter events, 313.1 us)
Async XLA Ops:
  7.2 384.3 %all-gather.2.cloned.1.call-start = ((), (), s32[]{:S(2)}) async-start(), calls=%async_computation | async-start | bytes 1052672 | tf_op jit(solution)/shard_map/all_gather | solution.py:108
  8.5 870.5 %all-reduce.7.cloned.1.call-start = ((), (), s32[]{:S(2)}) async-start(), calls=%async_computation.2 | async-start | bytes 2228224 | tf_op jit(solution)/shard_map/psum | solution.py:144
  8.6 11.9 collective-permute-start
  12.4 8.9 collective-permute-start.1
  21.4 3.5 collective-permute-start.2
  22.8 5.6 collective-permute-start.3
  441.2 3.7 copy-start.1
  492.4 3.7 copy-start.1
  543.8 3.7 copy-start.1
  577.9 3.7 copy-start.1
  595.1 3.7 copy-start.1
  599.6 18.5 %copy-start.2 = (f32[2,128,8,128]{3,1,0,2:T(8,128)S(1)}, f32[2,128,8,128]{3,1,0,2:T(8,128)}, u32[]{:S(2)}) copy-start(f32[2,128,8,128]{3,1,0,2:T(8,128)} %get-tuple-element.247) | copy-start | bytes 3145732
  600.7 12.5 collective-permute-start.4
  603.5 10.9 collective-permute-start.5
  615.5 4.5 collective-permute-start.6
  616.8 4.2 collective-permute-start.7
  619.9 260.0 %copy-start.13 = (f32[2,1024,128]{2,0,1:T(2,128)S(1)}, f32[2,1024,128]{2,0,1:T(2,128)}, u32[]{:S(2)}) copy-start(f32[2,1024,128]{2,0,1:T(2,128)} %all-gather.2.cloned.1.call-done) | copy-start | bytes 3145732
  619.9 726.8 %all-reduce.5.cloned.1.call-start = ((), (), s32[]{:S(2)}) async-start(), calls=%async_computation.1 | async-start | bytes 2228224 | tf_op jit(solution)/shard_map/psum | solution.py:144
  621.1 20.1 %copy-start.16 = (f32[2,64,64]{2,1,0:T(8,128)}, f32[2,64,64]{2,1,0:T(8,128)S(1)}, u32[]{:S(2)}) copy-start(f32[2,64,64]{2,1,0:T(8,128)S(1)} %fusion.68) | copy-start | bytes 98308
  621.1 9.9 collective-permute-start.8
  623.0 9.6 collective-permute-start.9
  632.6 5.3 collective-permute-start.10
  636.6 4.5 collective-permute-start.11
  927.6 3.7 copy-start.4
  976.8 3.7 copy-start.4
  1026.1 3.7 copy-start.4
  1058.9 3.7 copy-start.4
  1075.4 3.7 copy-start.4
  1081.0 12.5 collective-permute-start.12
  1082.9 10.7 collective-permute-start.13
  1094.6 2.7 collective-permute-start.14
  1095.9 4.4 collective-permute-start.15
  (164 other events, 190.3 us)
Sparse Core Ops, SparseCore 0:
  10.4 381.0 all-gather.1
  620.0 258.9 all-reduce.6
  1093.6 253.0 all-reduce.4
where the time goes:
time: 1360 us
  waiting for transfers between devices  861 us (63%)
  local copies, waits for them, and re-layouts  158 us (12%)
  other arithmetic  136 us (10%)
  loops' own time  88.1 us (6%)
  starting transfers between devices  51.3 us (4%)
  matrix products  46.9 us (3%)
  between operations  14.2 us (1%)
    psum x2, waiting for transfers between devices, local(): totals, weight_total = lax.psum((grad_rows, weight_probe), ('gy', 'gx'))  482 us
    all_gather x1, waiting for transfers between devices, local(): gathered = lax.all_gather(probe_modes, ('gy', 'gx'), axis=1, tiled=True)  362 us
    another operation x2, loops' own time, local(): lax.scan(visit, initial, (centres[:, 0], centres[:, 1], measured_all))  88.1 us
    dynamic_update_slice x24, local copies, waits for them, and re-layouts, visit(): lax.dynamic_update_slice(grad_obj, before + stacked, (zero_index, row_at,...  66.4 us
    add x48, other arithmetic, visit(): return ((grad_obj, grad_probe + g_probe, weight_probe + w_probe), None)  50.6 us
    while x336, local copies, waits for them, and re-layouts  49.5 us
    dot_general x48, matrix products, transform(): jnp.einsum('crmq,cqdk->drmk', halfway, right_op, preferred_element_type=j...  46.9 us
    sub x24, other arithmetic, position_terms(): shrink = 1.0 - measured / jnp.sqrt(intensity + SOFT_FLOOR)  35.8 us
  transfers between devices with their start and end apart: 19, of which 12 were waited for; matrix products, arithmetic and copies ran while one was open for 1% of the time, Pallas kernels for 0%

commit v1 on v0

--- a/solution.py
+++ b/solution.py
@@ -105,7 +105,10 @@
     measured_all = amplitudes.reshape(-1, probe_side, probe_side)
     forward = tables(probe_side, -1.0)
     inverse = tables(probe_side, 1.0)
-    gathered = lax.all_gather(probe_modes, ("gy", "gx"), axis=1, tiled=True)
+    gathered = jnp.concatenate(
+        lax.all_to_all(jnp.stack([probe_modes] * lax.axis_size(("gy", "gx"))), ("gy", "gx"), 0, 0),
+        axis=1,
+    )
     probe = unpack_probe(gathered, probe_side)
     own_rows = probe_modes
     current = object_field

time: 1360 us -> 1080 us (0.79)
  waiting for transfers between devices: 861 us -> 515 us
  local copies, waits for them, and re-layouts: 158 us -> 198 us
  starting transfers between devices: 51.3 us -> 68.8 us
    all_gather x1 -> x0, waiting for transfers between devices: 362 us -> none  [local(): gathered = lax.all_gather(probe_modes, ('gy', 'gx'), axis=1, tiled=True)]
    dynamic_slice x0 -> x48, local copies, waits for them, and re-layouts: none -> 22 us  [visit(): lax.dynamic_slice(grad_obj, (zero_index, row_at, col_at), (3, probe_side,...]
    dynamic_update_slice x24 -> x48, local copies, waits for them, and re-layouts: 66.4 us -> 82.3 us  [visit(): lax.dynamic_update_slice(grad_obj, before + stacked, (zero_index, row_at,...]
    while x336 -> x312, local copies, waits for them, and re-layouts: 49.5 us -> 34.1 us
    ppermute x4, waiting for transfers between devices: 0.31 us -> 15.5 us  [extended_2(): before = lax.ppermute(last, axis, up)]
    all_to_all x0 -> x1, starting transfers between devices: none -> 14.5 us  [local(): lax.all_to_all(jnp.stack([probe_modes] * lax.axis_size(('gy', 'gx'))), ('...]
where the time goes in v1:
time: 1080 us; the launch traced here: 1070 us
  waiting for transfers between devices  515 us (48%)
  local copies, waits for them, and re-layouts  198 us (18%)
  other arithmetic  128 us (12%)
  loops' own time  92.6 us (9%)
  starting transfers between devices  68.8 us (6%)
  matrix products  54.9 us (5%)
  between operations  14.5 us (1%)
    psum x2, waiting for transfers between devices, local(): totals, weight_total = lax.psum((grad_rows, weight_probe), ('gy', 'gx'))  482 us
    another operation x2, loops' own time, local(): lax.scan(visit, initial, (centres[:, 0], centres[:, 1], measured_all))  92.6 us
    dynamic_update_slice x48, local copies, waits for them, and re-layouts, visit(): lax.dynamic_update_slice(grad_obj, before + stacked, (zero_index, row_at,...  82.3 us
    dot_general x48, matrix products, transform(): jnp.einsum('crmq,cqdk->drmk', halfway, right_op, preferred_element_type=j...  54.9 us
    add x48, other arithmetic, visit(): return ((grad_obj, grad_probe + g_probe, weight_probe + w_probe), None)  53.1 us
    sub x24, other arithmetic, position_terms(): shrink = 1.0 - measured / jnp.sqrt(intensity + SOFT_FLOOR)  35.3 us
    while x312, local copies, waits for them, and re-layouts  34.1 us
    dynamic_slice x48, local copies, waits for them, and re-layouts, local(): lax.scan(visit, initial, (centres[:, 0], centres[:, 1], measured_all))  31.2 us
  transfers between devices with their start and end apart: 19, of which 12 were waited for; matrix products, arithmetic and copies ran while one was open for 1% of the time, Pallas kernels for 0%

profile of v1, /device:TPU:16, one launch (start us, length us, event | category | flops | bytes accessed | tf_op | source)
XLA Modules:
  0.0 1071.6 jit_solution(2636483579199690247)
XLA Ops:
  9.0 14.5 %all-to-all-start = ((f32[256,2,4,128]{3,2,1,0:T(4,128)}), f32[256,2,4,128]{3,2,1,0:T(4,128)S(1)}, u32[]{:S(2)}, u32[]{:S(2)}) async-start(f32[256,2,4,128]{3,2,1,0:T(4,128)} %stack.80), calls=%async_computation | async-start | bytes 2097152 | tf_op jit(solution)/shard_map/all_to_all | solution.py:109
  23.6 3.6 collective-permute-start
  27.2 5.8 collective-permute-start.1
  35.9 15.2 %collective-permute-done = f32[2,64,64]{1,2,0:T(8,128)S(1)} collective-permute-done((f32[2,64,64]{1,2,0:T(8,128)S(1)}, f32[2,64,64]{1,2,0:T(8,128)S(1)}, u32[]{:S(2)}, u32[]{:S(2)}) %collective-permute-start) | collective-permute-done | bytes 32800 | tf_op jit(solution)/shard_map/ppermute | solution.py:27
  54.5 3.5 collective-permute-done.3
  61.7 225.8 %while.38 = (s32[]{:T(128)}, f32[3,192,192]{2,1,0:T(8,128)}, f32[2,128,8,128]{1,3,0,2:T(8,128)}, f32[128,128]{0,1:T(8,128)}, s32[12]{0:T(128)S(1)}, /*index=5*/s...) while((s32[]{:T(128)}, f32[3,192,192]{2,1,0:T(8,128)}, ...), condition=%wide.region_5.6_spmd.clone, body=%wide.region_1.5_spmd.clone.sunk | while | flops 543391744 | bytes 25559488 | solution.py:141
  76.6 3.7 dynamic_update_slice.10
  95.4 3.8 dynamic_update_slice.10
  114.1 3.9 dynamic_update_slice.10
  133.1 3.8 dynamic_update_slice.10
  151.8 3.7 dynamic_update_slice.10
  170.6 3.9 dynamic_update_slice.10
  189.5 3.8 dynamic_update_slice.10
  208.3 3.8 dynamic_update_slice.10
  227.1 3.9 dynamic_update_slice.10
  246.0 3.7 dynamic_update_slice.10
  264.7 3.9 dynamic_update_slice.10
  283.6 3.9 dynamic_update_slice.10
  290.6 7.5 collective-permute-start.5
  302.3 4.3 collective-permute-start.6
  309.3 2.8 collective-permute-done.7
  314.9 7.5 collective-permute-start.9
  324.4 4.2 collective-permute-start.10
  333.7 237.3 %all-reduce.7.cloned.1.call-done = (f32[2,1024,128]{2,1,0:T(8,128)}, f32[128,128]{0,1:T(8,128)}) async-done(((f32[2,1024,128]{2,1,0:T(8,128)}, f32[128,128]{0,1:T(8,128)}), (f32[2,1024,128]{2,1,0:T(8,128)}, f32[128,128]{0,1:T(8,128)})) %all-reduce.7.cloned.1.call-update) | async-done | bytes 1114128 | tf_op jit(solution)/shard_map/psum | solution.py:147
  575.4 220.6 %while.39 = (s32[]{:T(128)}, f32[3,192,192]{2,1,0:T(8,128)}, f32[2,128,8,128]{1,3,0,2:T(8,128)}, f32[128,128]{0,1:T(8,128)}, s32[12]{0:T(128)S(1)}, /*index=5*/s...) while((s32[]{:T(128)}, f32[3,192,192]{2,1,0:T(8,128)}, ...), condition=%wide.region_13.14_spmd.clone, body=%wide.region_9.13_spmd.clone.sunk | while | flops 543391744 | bytes 21627380 | solution.py:141
  625.9 2.8 dynamic_update_slice.11
  681.3 2.8 dynamic_update_slice.11
  736.8 2.8 dynamic_update_slice.11
  773.8 2.9 dynamic_update_slice.11
  799.0 7.5 collective-permute-start.13
  813.4 3.0 collective-permute-done.15
  817.9 244.5 %all-reduce.5.cloned.1.call-done = (f32[2,1024,128]{2,1,0:T(8,128)}, f32[128,128]{0,1:T(8,128)}) async-done(((f32[2,1024,128]{2,1,0:T(8,128)}, f32[128,128]{0,1:T(8,128)}), (f32[2,1024,128]{2,1,0:T(8,128)}, f32[128,128]{0,1:T(8,128)})) %all-reduce.5.cloned.1.call-update) | async-done | bytes 1114128 | tf_op jit(solution)/shard_map/psum | solution.py:147
  (768 shorter events, 345.8 us)
Async XLA Ops:
  9.0 14.6 %copy-start.19 = (f32[2,64,64]{2,1,0:T(8,128)S(1)}, f32[2,64,64]{2,1,0:T(8,128)}, u32[]{:S(2)}) copy-start(f32[2,64,64]{2,1,0:T(8,128)} %param.24) | copy-start | bytes 98308
  9.0 49.9 %all-to-all-start = ((f32[256,2,4,128]{3,2,1,0:T(4,128)}), f32[256,2,4,128]{3,2,1,0:T(4,128)S(1)}, u32[]{:S(2)}, u32[]{:S(2)}) async-start(f32[256,2,4,128]{3,2,1,0:T(4,128)} %stack.80), calls=%async_computation | async-start | bytes 2097152 | tf_op jit(solution)/shard_map/all_to_all | solution.py:109
  23.5 547.5 %all-reduce.7.cloned.1.call-start = ((), (), s32[]{:S(2)}) async-start(), calls=%async_computation.2 | async-start | bytes 2228224 | tf_op jit(solution)/shard_map/psum | solution.py:147
  23.6 27.5 %collective-permute-start = (f32[2,64,64]{1,2,0:T(8,128)S(1)}, f32[2,64,64]{1,2,0:T(8,128)S(1)}, u32[]{:S(2)}, u32[]{:S(2)}) collective-permute-start(f32[2,64,64]{1,2,0:T(8,128)S(1)} %copy.113), channel_id=1, source_target_pairs={{0,1},{1,2},{2,3},{3,4},{4,5},{5,6},{6,7},{7,8},{8,9},{9,10},{10,1... | collective-permute-start | bytes 98312 | tf_op jit(solution)/shard_map/ppermute | solution.py:27
  27.2 23.9 %collective-permute-start.1 = (f32[2,64,64]{1,2,0:T(8,128)S(1)}, f32[2,64,64]{1,2,0:T(8,128)S(1)}, u32[]{:S(2)}, u32[]{:S(2)}) collective-permute-start(f32[2,64,64]{1,2,0:T(8,128)S(1)} %copy.113), channel_id=1, source_target_pairs={{1,0},{2,1},{3,2},{4,3},{5,4},{6,5},{7,6},{8,7},{9,8},{10,9},{11,1... | collective-permute-start | bytes 98312 | tf_op jit(solution)/shard_map/ppermute | solution.py:28
  51.2 3.3 collective-permute-start.2
  52.5 5.5 collective-permute-start.3
  92.8 6.3 copy-start.1
  111.6 6.5 copy-start.1
  130.5 6.3 copy-start.1
  168.0 6.5 copy-start.1
  186.9 6.4 copy-start.1
  205.8 6.3 copy-start.1
  224.6 6.5 copy-start.1
  262.1 6.5 copy-start.1
  281.1 6.5 copy-start.1
  287.5 20.4 %copy-start.2 = (f32[2,128,8,128]{1,3,0,2:T(8,128)S(1)}, f32[2,128,8,128]{1,3,0,2:T(8,128)}, u32[]{:S(2)}) copy-start(f32[2,128,8,128]{1,3,0,2:T(8,128)} %get-tuple-element.247) | copy-start | bytes 3145732
  288.7 11.2 %collective-permute-start.4 = (f32[3,64,192]{2,1,0:T(8,128)S(1)}, f32[3,64,192]{2,1,0:T(8,128)S(1)}, u32[]{:S(2)}, u32[]{:S(2)}) collective-permute-start(f32[3,64,192]{2,1,0:T(8,128)S(1)} %get-tuple-element.593), channel_id=1, source_target_pairs={{0,1},{1,2},{2,3},{3,4},{4,5},{5,6},{6,7},{7,8},{8,9},{9,10},{10,1... | collective-permute-start | bytes 442376 | tf_op jit(solution)/shard_map/ppermute | solution.py:17
  290.6 10.7 collective-permute-start.5
  302.3 7.0 collective-permute-start.6
  306.6 5.5 collective-permute-start.7
  309.3 753.2 %all-reduce.5.cloned.1.call-start = ((), (), s32[]{:S(2)}) async-start(), calls=%async_computation.1 | async-start | bytes 2228224 | tf_op jit(solution)/shard_map/psum | solution.py:147
  312.2 259.7 %copy-start.4 = (f32[2,256,4,128]{3,2,1,0:T(4,128)S(1)}, f32[2,256,4,128]{3,2,1,0:T(4,128)}, u32[]{:S(2)}) copy-start(f32[2,256,4,128]{3,2,1,0:T(4,128)} %copy-done.3) | copy-start | bytes 3145732
  313.0 19.8 %copy-start.15 = (f32[2,64,64]{2,1,0:T(8,128)}, f32[2,64,64]{2,1,0:T(8,128)S(1)}, u32[]{:S(2)}) copy-start(f32[2,64,64]{2,1,0:T(8,128)S(1)} %fusion.67) | copy-start | bytes 98308
  313.0 9.8 collective-permute-start.8
  314.9 9.4 collective-permute-start.9
  324.4 5.7 collective-permute-start.10
  328.5 4.2 collective-permute-start.11
  797.0 12.0 %collective-permute-start.12 = (f32[3,64,192]{2,1,0:T(8,128)S(1)}, f32[3,64,192]{2,1,0:T(8,128)S(1)}, u32[]{:S(2)}, u32[]{:S(2)}) collective-permute-start(f32[3,64,192]{2,1,0:T(8,128)S(1)} %get-tuple-element.591), channel_id=1, source_target_pairs={{0,1},{1,2},{2,3},{3,4},{4,5},{5,6},{6,7},{7,8},{8,9},{9,10},{10,1... | collective-permute-start | bytes 442376 | tf_op jit(solution)/shard_map/ppermute | solution.py:17
  799.0 10.7 collective-permute-start.13
  810.7 2.7 collective-permute-start.14
  812.0 4.4 collective-permute-start.15
  (141 other events, 184.0 us)
Sparse Core Ops, SparseCore 0:
  309.4 261.5 all-reduce.6
  809.2 253.2 all-reduce.4
